TPU v7x, 128 devices: a whole 4x4x4 slice. The times are simulated.
128 devices in a mesh: ma: 32 (over z, x, core), band: 4 (over y).
Axes of the slice: x: 4, y: 4, z: 4, core: 2. Of those that a mesh axis runs over, the one named last changes fastest.
Arguments:
- observed: bfloat16 [1024, 64, 1024], P(('ma', 'band')), may hold values from -6 to 6
- eigenvalues: float32 [1024, 1024], P(('ma', 'band')), may hold values from 0.05 to 20
- kl_basis: bfloat16 [1024, 1024, 512], P(('ma', 'band')), may hold values from -0.1875 to 0.1875
- band_deriv: bfloat16 [40, 512, 512], P('band'), may hold values from -0.15625 to 0.15625, as said below
- counts: int32 [1024], P(('ma', 'band')), may hold values from 128 to 1024, as said below
Outputs:
- mode_power: float32 [1024, 40], P('ma', 'band')
- band_power: float32 [40], P('band')
Inputs may be any that keep to these rules, and one draw needn't show every extreme that they name: counts[m] is the number of leading KL modes of m-mode m that are kept; some m-mode keeps 1024 and some keeps 1024 // 8. Each band_deriv[a] is symmetric.
All inputs are finite; a program needn't handle non-finite values.
Results may differ from a plain program's by a relative error of at most 0.0018.
Values may be sent and summed in bfloat16 or wider, within the bound.
A program may use at most 64 MiB of HBM per device.

v0:
```python
import jax
import jax.numpy as jnp
from jax import lax
from jax.sharding import Mesh
from jax.sharding import PartitionSpec as P

MA_BAND = ("ma_0", "ma_1", "ma_2", "band")
MA = ("ma_0", "ma_1", "ma_2")


def from_everyone(x, axis):
    count = lax.axis_size(axis)
    return lax.all_to_all(jnp.broadcast_to(x[None], (count, *x.shape)), axis, 0, 0, tiled=True)


def laid_out(tiles, dim):
    tiles = jnp.moveaxis(tiles, 0, dim)
    shape = tiles.shape
    return tiles.reshape(*shape[:dim], shape[dim] * shape[dim + 1], *shape[dim + 2 :])


def gather_directly(x, axis, dim):
    tiles = from_everyone(x, axis)
    return laid_out(tiles, dim)


def over_axes(x, axes):
    for axis in axes:
        x = lax.psum(x, axis)
    return x


def weigh(observed, eigenvalues, counts):
    position = lax.broadcasted_iota(jnp.int32, eigenvalues.shape, 1)
    inside = position < counts[:, None]
    weights = jnp.where(inside, 1.0 / (1.0 + eigenvalues), jnp.zeros_like(eigenvalues))
    return (observed.astype(jnp.float32) * weights[:, None, :]).astype(jnp.bfloat16)


def project_padded(weighted, kl_basis):
    return jnp.einsum("msi,miw->msw", weighted, kl_basis, preferred_element_type=jnp.float32)


def band_quadratic(vectors, matrices):
    mode_count = vectors.shape[0]
    flattened = vectors.reshape(mode_count * vectors.shape[1], vectors.shape[2])

    def one_band(matrix):
        mapped = jnp.dot(flattened, matrix, preferred_element_type=jnp.float32)
        return jnp.sum((mapped * flattened).reshape(mode_count, -1), axis=1)

    return lax.map(one_band, matrices)


def per_device(observed, eigenvalues, kl_basis, band_deriv, counts):
    samples = observed.shape[1]
    own_bands = band_deriv.shape[0]
    weighted = weigh(observed, eigenvalues, counts)
    projected = project_padded(weighted, kl_basis)
    projected = projected.astype(jnp.bfloat16)
    quadratic = band_quadratic(gather_directly(projected, "band", 0), band_deriv)
    mode_power = jnp.transpose(quadratic) / samples
    partial_sum = jnp.sum(mode_power, axis=0)
    band_start = lax.axis_index("band") * own_bands
    scattered = jnp.zeros((own_bands * lax.axis_size("band"),), jnp.float32)
    scattered = lax.dynamic_update_slice_in_dim(scattered, partial_sum, band_start, 0)
    every_band, live_total = (
        over_axes(scattered, MA_BAND),
        over_axes(jnp.sum(counts).astype(jnp.float32), MA_BAND),
    )
    band_total = lax.dynamic_slice_in_dim(every_band, band_start, own_bands, 0)
    band_power = observed.shape[2] * band_total / live_total
    return (mode_power, band_power)


def solution(mesh):
    split = Mesh(
        mesh.devices.reshape(4, 4, 2, mesh.shape["band"]), ("ma_0", "ma_1", "ma_2", "band")
    )
    return jax.shard_map(
        per_device,
        mesh=split,
        in_specs=(
            P(MA_BAND, None, None),
            P(MA_BAND, None),
            P(MA_BAND, None, None),
            P("band", None, None),
            P(MA_BAND),
        ),
        out_specs=(P(MA, "band"), P("band")),
        check_vma=False,
    )
```

profile of v0, /device:TPU:1, one launch (start us, length us, event | category | flops | bytes accessed | tf_op | source)
XLA Modules:
  0.0 118.2 jit_solution(1673569421186196398)
XLA Ops:
  0.6 0.8 divide_select_fusion
  1.5 5.2 %convolution_convert_fusion = bf16[8,64,512]{2,1,0:T(8,128)(2,1)S(1)} fusion(bf16[8,1024,512]{2,1,0:T(8,128)(2,1)} %param.9, bf16[8,64,1024]{2,1,0:T(8,128)(2,1)} %param.7, f32[8,1024]{1,0:T(8,128)S(1)} %divide_select_fusion), kind=kOutput, calls=%fused_computation.6 | convolution fusion | flops 538705920 | bytes 9994240 | tf_op jit(solution)/shard_map/msi,miw->msw/dot_general | solution.py:41
  6.7 1.6 %broadcast_in_dim.23 = bf16[4,8,64,512]{3,2,1,0:T(8,128)(2,1)} broadcast(bf16[8,64,512]{2,1,0:T(8,128)(2,1)S(1)} %convolution_convert_fusion), dimensions={1,2,3} | broadcast | bytes 2621440 | tf_op jit(solution)/shard_map/broadcast_in_dim | solution.py:13
  8.3 5.0 %all-to-all-start = ((bf16[4,8,64,512]{3,2,1,0:T(8,128)(2,1)}), bf16[4,8,64,512]{3,2,1,0:T(8,128)(2,1)S(1)}, u32[]{:S(2)}, u32[]{:S(2)}) async-start(bf16[4,8,64,512]{3,2,1,0:T(8,128)(2,1)} %broadcast_in_dim.23), calls=%async_computation | async-start | bytes 4194304 | tf_op jit(solution)/shard_map/all_to_all | solution.py:13
  13.3 0.6 reduce_sum.35
  14.6 24.2 %all-to-all-done = bf16[4,8,64,512]{3,2,1,0:T(8,128)(2,1)S(1)} async-done(((bf16[4,8,64,512]{3,2,1,0:T(8,128)(2,1)}), bf16[4,8,64,512]{3,2,1,0:T(8,128)(2,1)S(1)}, u32[]{:S(2)}, u32[]{:S(2)}) %all-to-all-start) | async-done | bytes 2097184 | tf_op jit(solution)/shard_map/all_to_all | solution.py:13
  38.8 2.5 %copy.9 = bf16[2048,512]{0,1:T(8,128)(2,1)} copy(bf16[2048,512]{1,0:T(8,128)(2,1)S(1)} %bitcast.21) | data formatting | bytes 4194304 | tf_op jit(solution)/shard_map/while | solution.py:52
  41.2 39.3 %while.10 = (s32[]{:T(128)}, f32[10,32]{1,0:T(8,128)S(1)}, bf16[10,512,512]{2,1,0:T(8,128)(2,1)}, bf16[2048,512]{0,1:T(8,128)(2,1)}, s32[]{:T(128)}, /*index=5*/f32[]{:T(128)}, s32[]{:T(128)}) while((s32[]{:T(128)}, f32[10,32]{1,0:T(8,128)S(1)}, bf16[10,512,512]{2,1,0:T(8,128)(2,1)}, bf16[2048,512]{0,1:T(8,128)(2,1)}, s32[]{:T(128)}, ...), condition=%wide.region_3.4_spmd, body=%wide.region_0.3_spmd.sunk | while | flops 1076887552 | bytes 4752341 | solution.py:52
  41.2 3.7 %fusion.12 = f32[2048]{0:T(1024)S(1)} fusion(bf16[2048,512]{0,1:T(8,128)(2,1)} %get-tuple-element.93, bf16[10,512,512]{2,1,0:T(8,128)(2,1)} %get-tuple-element.92, s32[]{:T(128)} %get-tuple-element.83), kind=kOutput, calls=%fused_computation.1.clone.1 | convolution fusion | flops 1076885504 | bytes 4727296 | tf_op jit(solution)/shard_map/while/body/eval_jaxpr/dot_general | solution.py:49
  45.2 3.7 %fusion.12 = f32[2048]{0:T(1024)S(1)} fusion(bf16[2048,512]{0,1:T(8,128)(2,1)} %get-tuple-element.93, bf16[10,512,512]{2,1,0:T(8,128)(2,1)} %get-tuple-element.92, s32[]{:T(128)} %get-tuple-element.83), kind=kOutput, calls=%fused_computation.1.clone.1 | convolution fusion | flops 1076885504 | bytes 4727296 | tf_op jit(solution)/shard_map/while/body/eval_jaxpr/dot_general | solution.py:49
  49.1 3.7 %fusion.12 = f32[2048]{0:T(1024)S(1)} fusion(bf16[2048,512]{0,1:T(8,128)(2,1)} %get-tuple-element.93, bf16[10,512,512]{2,1,0:T(8,128)(2,1)} %get-tuple-element.92, s32[]{:T(128)} %get-tuple-element.83), kind=kOutput, calls=%fused_computation.1.clone.1 | convolution fusion | flops 1076885504 | bytes 4727296 | tf_op jit(solution)/shard_map/while/body/eval_jaxpr/dot_general | solution.py:49
  53.0 3.7 %fusion.12 = f32[2048]{0:T(1024)S(1)} fusion(bf16[2048,512]{0,1:T(8,128)(2,1)} %get-tuple-element.93, bf16[10,512,512]{2,1,0:T(8,128)(2,1)} %get-tuple-element.92, s32[]{:T(128)} %get-tuple-element.83), kind=kOutput, calls=%fused_computation.1.clone.1 | convolution fusion | flops 1076885504 | bytes 4727296 | tf_op jit(solution)/shard_map/while/body/eval_jaxpr/dot_general | solution.py:49
  56.9 3.7 %fusion.12 = f32[2048]{0:T(1024)S(1)} fusion(bf16[2048,512]{0,1:T(8,128)(2,1)} %get-tuple-element.93, bf16[10,512,512]{2,1,0:T(8,128)(2,1)} %get-tuple-element.92, s32[]{:T(128)} %get-tuple-element.83), kind=kOutput, calls=%fused_computation.1.clone.1 | convolution fusion | flops 1076885504 | bytes 4727296 | tf_op jit(solution)/shard_map/while/body/eval_jaxpr/dot_general | solution.py:49
  60.9 3.7 %fusion.12 = f32[2048]{0:T(1024)S(1)} fusion(bf16[2048,512]{0,1:T(8,128)(2,1)} %get-tuple-element.93, bf16[10,512,512]{2,1,0:T(8,128)(2,1)} %get-tuple-element.92, s32[]{:T(128)} %get-tuple-element.83), kind=kOutput, calls=%fused_computation.1.clone.1 | convolution fusion | flops 1076885504 | bytes 4727296 | tf_op jit(solution)/shard_map/while/body/eval_jaxpr/dot_general | solution.py:49
  64.8 3.7 %fusion.12 = f32[2048]{0:T(1024)S(1)} fusion(bf16[2048,512]{0,1:T(8,128)(2,1)} %get-tuple-element.93, bf16[10,512,512]{2,1,0:T(8,128)(2,1)} %get-tuple-element.92, s32[]{:T(128)} %get-tuple-element.83), kind=kOutput, calls=%fused_computation.1.clone.1 | convolution fusion | flops 1076885504 | bytes 4727296 | tf_op jit(solution)/shard_map/while/body/eval_jaxpr/dot_general | solution.py:49
  68.7 3.7 %fusion.12 = f32[2048]{0:T(1024)S(1)} fusion(bf16[2048,512]{0,1:T(8,128)(2,1)} %get-tuple-element.93, bf16[10,512,512]{2,1,0:T(8,128)(2,1)} %get-tuple-element.92, s32[]{:T(128)} %get-tuple-element.83), kind=kOutput, calls=%fused_computation.1.clone.1 | convolution fusion | flops 1076885504 | bytes 4727296 | tf_op jit(solution)/shard_map/while/body/eval_jaxpr/dot_general | solution.py:49
  72.7 3.7 %fusion.12 = f32[2048]{0:T(1024)S(1)} fusion(bf16[2048,512]{0,1:T(8,128)(2,1)} %get-tuple-element.93, bf16[10,512,512]{2,1,0:T(8,128)(2,1)} %get-tuple-element.92, s32[]{:T(128)} %get-tuple-element.83), kind=kOutput, calls=%fused_computation.1.clone.1 | convolution fusion | flops 1076885504 | bytes 4727296 | tf_op jit(solution)/shard_map/while/body/eval_jaxpr/dot_general | solution.py:49
  76.6 3.7 %fusion.12 = f32[2048]{0:T(1024)S(1)} fusion(bf16[2048,512]{0,1:T(8,128)(2,1)} %get-tuple-element.93, bf16[10,512,512]{2,1,0:T(8,128)(2,1)} %get-tuple-element.92, s32[]{:T(128)} %get-tuple-element.83), kind=kOutput, calls=%fused_computation.1.clone.1 | convolution fusion | flops 1076885504 | bytes 4727296 | tf_op jit(solution)/shard_map/while/body/eval_jaxpr/dot_general | solution.py:49
  80.5 0.7 multiply_reduce_fusion
  81.5 10.2 %all-reduce.2 = (f32[40]{0:T(128)S(1)}, f32[]{:T(128)}) all-reduce(f32[40]{0:T(128)S(1)} %dynamic_update_slice.7, f32[]{:T(128)S(6)} %convert_element_type.18), channel_id=1, replica_groups=mesh['ma_0'=4,'ma_1'=4,'ma_2'=2,'band'=4] {'ma_0'}, use_global_device_ids=true, to_apply=%region_5.6 | all-reduce | flops 41 | bytes 328 | tf_op jit(solution)/shard_map/psum | solution.py:29
  91.7 9.1 %all-reduce.1 = (f32[40]{0:T(128)S(1)}, f32[]{:T(128)}) all-reduce(f32[40]{0:T(128)S(1)} %get-tuple-element.45, f32[]{:T(128)} %get-tuple-element.46), channel_id=1, replica_groups=mesh['ma_0'=4,'ma_1'=4,'ma_2'=2,'band'=4] {'ma_1'}, use_global_device_ids=true, to_apply=%region_6.7 | all-reduce | flops 41 | bytes 328 | tf_op jit(solution)/shard_map/psum | solution.py:29
  100.8 8.6 %all-reduce.3 = (f32[40]{0:T(128)S(1)}, f32[]{:T(128)}) all-reduce(f32[40]{0:T(128)S(1)} %get-tuple-element.43, f32[]{:T(128)} %get-tuple-element.44), channel_id=1, replica_groups=mesh['ma_0'=4,'ma_1'=4,'ma_2'=2,'band'=4] {'ma_2'}, use_global_device_ids=true, to_apply=%region_7.8 | all-reduce | flops 41 | bytes 328 | tf_op jit(solution)/shard_map/psum | solution.py:29
  109.4 7.6 %all-reduce = (f32[40]{0:T(128)S(1)}, f32[]{:T(128)}) all-reduce(f32[40]{0:T(128)S(1)} %get-tuple-element.47, f32[]{:T(128)} %get-tuple-element.48), channel_id=1, replica_groups=mesh['ma_0'=4,'ma_1'=4,'ma_2'=2,'band'=4] {'band'}, use_global_device_ids=true, to_apply=%region_8.9 | all-reduce | flops 41 | bytes 328 | tf_op jit(solution)/shard_map/psum | solution.py:29
  116.9 1.3 %multiply_divide_fusion = f32[10]{0:T(128)} fusion(f32[40]{0:T(128)S(1)} %get-tuple-element.41, s32[]{:T(128)S(6)} %select_n.9, f32[]{:T(128)} %get-tuple-element.42), kind=kLoop, calls=%fused_computation.12 | loop fusion | flops 20 | bytes 88 | tf_op jit(solution)/shard_map/div | solution.py:72
  (35 shorter events, 2.5 us)
Async XLA Ops:
  6.7 6.6 %copy-start = (s32[8]{0:T(128)S(1)}, s32[8]{0:T(128)}, u32[]{:S(2)}) copy-start(s32[8]{0:T(128)} %param.11) | copy-start | bytes 100
  8.3 30.5 %all-to-all-start = ((bf16[4,8,64,512]{3,2,1,0:T(8,128)(2,1)}), bf16[4,8,64,512]{3,2,1,0:T(8,128)(2,1)S(1)}, u32[]{:S(2)}, u32[]{:S(2)}) async-start(bf16[4,8,64,512]{3,2,1,0:T(8,128)(2,1)} %broadcast_in_dim.23), calls=%async_computation | async-start | bytes 4194304 | tf_op jit(solution)/shard_map/all_to_all | solution.py:13
where the time goes:
time: 120 us; the launch traced here: 118 us
  matrix products  42.1 us (35%)
  blocking collectives  35.5 us (30%)
  waiting for transfers between devices  24.2 us (20%)
  local copies, waits for them, and re-layouts  5.36 us (4%)
  starting transfers between devices  5 us (4%)
  other arithmetic  4.61 us (4%)
  between operations  1.31 us (1%)
    dot_general x10, matrix products, one_band(): mapped = jnp.dot(flattened, matrix, preferred_element_type=jnp.float32)  36.9 us
    psum x4, blocking collectives, over_axes(): x = lax.psum(x, axis)  35.5 us
    all_to_all x1, waiting for transfers between devices, from_everyone(): lax.all_to_all(jnp.broadcast_to(x[None], (count, *x.shape)), axis, 0, 0,...  24.2 us
    dot_general x1, matrix products, project_padded(): jnp.einsum('msi,miw->msw', weighted, kl_basis, preferred_element_type=jnp...  5.22 us
    all_to_all x1, starting transfers between devices, from_everyone(): lax.all_to_all(jnp.broadcast_to(x[None], (count, *x.shape)), axis, 0, 0,...  5 us
    while x1, local copies, waits for them, and re-layouts, band_quadratic(): return lax.map(one_band, matrices)  2.47 us
  transfers between devices with their start and end apart: 1, of which 1 were waited for; matrix products, arithmetic and copies ran while one was open for 1% of the time, Pallas kernels for 0%

commit v1 on v0

v1 whole, which is shorter than its diff:
```python
import functools

import jax
import jax.numpy as jnp
from jax import lax
from jax.experimental import pallas as pl
from jax.experimental.pallas import tpu as pltpu
from jax.sharding import Mesh
from jax.sharding import PartitionSpec as P

MA = ("ma_0", "ma_1", "ma_2")
MA_BAND = MA + ("band",)
MESH = pl.DeviceIdType.MESH
LANES = 128
F32 = jnp.float32
BF16 = jnp.bfloat16


def kernel(
    counts_hbm, eig_hbm, obs_hbm, kl_hbm, d_hbm,
    mode_ref, power_ref,
    counts_s, eig_v, weight_v, obs_v, kl_v, d1_v, d2_v, vec, acc, tiles, row_c, rows,
    small_sem, obs_sem, kl_sem, d_sem, send_sem, recv_sem, csend_sem, crecv_sem, rsend_sem, rrecv_sem,
):
    own, samples, nmax = obs_v.shape
    bands, width, half = d1_v.shape
    depth = lax.axis_size("band")
    z, x, core = (lax.axis_index(a) for a in MA)
    nz, nx, nc = (lax.axis_size(a) for a in MA)
    plane = nz * nx * nc
    me = (z * nx + x) * nc + core
    y = lax.axis_index("band")
    right = lax.rem(y + 1, depth)
    left = lax.rem(y + depth - 1, depth)

    def peer(d):
        t = lax.rem(me + d, plane)
        return {"ma_0": t // (nx * nc), "ma_1": lax.rem(t // nc, nx), "ma_2": lax.rem(t, nc)}

    counts_cp = pltpu.make_async_copy(counts_hbm, counts_s, small_sem.at[0])
    eig_cp = pltpu.make_async_copy(eig_hbm, eig_v, small_sem.at[1])
    counts_cp.start()
    eig_cp.start()

    def obs_cp(m):
        return pltpu.make_async_copy(obs_hbm.at[m], obs_v.at[m], obs_sem.at[m])

    def kl_cp(m):
        return pltpu.make_async_copy(kl_hbm.at[m], kl_v.at[m], kl_sem.at[m])

    @pl.loop(0, own)
    def _(m):
        obs_cp(m).start()
        kl_cp(m).start()

    d1_cp = pltpu.make_async_copy(d_hbm.at[:, :, pl.ds(0, half)], d1_v, d_sem.at[0])
    d2_cp = pltpu.make_async_copy(d_hbm.at[:, pl.ds(half, half), pl.ds(half, half)], d2_v, d_sem.at[1])
    d1_cp.start()
    d2_cp.start()

    barrier = pltpu.get_barrier_semaphore()
    for n in (left, right):
        pl.semaphore_signal(barrier, inc=1, device_id={"band": n}, device_id_type=MESH)

    @pl.loop(1, plane)
    def _(d):
        pl.semaphore_signal(barrier, inc=1, device_id=peer(d), device_id_type=MESH)

    counts_cp.wait()
    eig_cp.wait()
    sub = lax.broadcasted_iota(jnp.int32, (own, nmax), 0)
    pos = lax.broadcasted_iota(jnp.int32, (own, nmax), 1)
    limit = jnp.zeros((own, nmax), jnp.int32)
    total = counts_s[0]
    for m in range(own):
        limit = jnp.where(sub == m, counts_s[m], limit)
        if m:
            total = total + counts_s[m]
    weight_v[...] = jnp.where(pos < limit, 1.0 / (1.0 + eig_v[...]), 0.0)
    row_c[0] = jnp.full((1, LANES), total.astype(F32))

    pl.semaphore_wait(barrier, plane + 1)

    def remote(src, dst, s, r, n):
        return pltpu.make_async_remote_copy(
            src_ref=src, dst_ref=dst, send_sem=s, recv_sem=r, device_id={"band": n}, device_id_type=MESH
        )

    def e_left(m):
        return 8 + (m // 4) * 8 + lax.rem(m, 4)

    def e_right(m):
        return 12 + (m // 4) * 8 + lax.rem(m, 4)

    def e_far_l(m):
        return 24 + (m // 2) * 4 + lax.rem(m, 2)

    def e_far_r(m):
        return 26 + (m // 2) * 4 + lax.rem(m, 2)

    def to_right(m):
        return remote(vec.at[m], vec.at[e_left(m)], send_sem.at[0, m], recv_sem.at[e_left(m)], right)

    def to_left(m):
        return remote(vec.at[m], vec.at[e_right(m)], send_sem.at[1, m], recv_sem.at[e_right(m)], left)

    def on_right(m):
        return remote(vec.at[e_left(m)], vec.at[e_far_l(m)], send_sem.at[0, 8 + m], recv_sem.at[e_far_l(m)], right)

    def on_left(m):
        e = e_right(m + 4)
        return remote(vec.at[e], vec.at[e_far_r(m)], send_sem.at[1, 8 + m], recv_sem.at[e_far_r(m)], left)

    def c_copy(s, d, k, n):
        return remote(row_c.at[s], row_c.at[d], csend_sem.at[k], crecv_sem.at[d], n)

    @pl.loop(0, own)
    def _(m):
        obs_cp(m).wait()
        kl_cp(m).wait()
        weighted = (obs_v[m].astype(F32) * weight_v[pl.ds(m, 1), :]).astype(BF16)
        vec[m] = jnp.dot(weighted, kl_v[m], preferred_element_type=F32).astype(BF16)
        to_right(m).start()
        to_left(m).start()

    c_copies = (c_copy(0, 1, 0, right), c_copy(0, 2, 1, left), c_copy(1, 3, 2, right))
    c_copies[0].start()
    c_copies[1].start()

    d1_cp.wait()
    d2_cp.wait()

    @pl.loop(0, bands)
    def _(a):
        d1_v[a, half:, :] = d1_v[a, half:, :] * 2

    def band_products(e0, n):
        @pl.loop(0, bands)
        def _(a):
            p = vec[e0 : e0 + n].reshape(n * samples, width)
            y1 = jnp.dot(p, d1_v[a], preferred_element_type=F32)
            y2 = jnp.dot(p[:, half:], d2_v[a], preferred_element_type=F32)
            q = y1 * p[:, :half].astype(F32) + y2 * p[:, half:].astype(F32)
            q = q[:, :LANES] + q[:, LANES:]
            q = jnp.sum(q.reshape(n, samples // 8, 8, LANES), axis=1)
            acc[a, e0 * 8 : (e0 + n) * 8, :] = q.reshape(n * 8, LANES)

    lane = lax.broadcasted_iota(jnp.int32, (8, LANES), 1)

    def gather_tile(g):
        t = jnp.zeros((8, LANES), F32)
        for a in range(bands):
            v = acc[a, pl.ds(g * 64, 8, stride=8), :]
            for k in range(1, 8):
                v = v + acc[a, pl.ds(g * 64 + k, 8, stride=8), :]
            t = jnp.where(lane == a, jnp.sum(v, axis=1, keepdims=True), t)
        t = t / samples
        tiles[g] = t

    band_products(0, 8)
    gather_tile(0)

    c_copies[0].wait_recv()
    c_copies[2].start()
    for m in range(4):
        to_right(m).wait_recv()
        on_right(m).start()
        to_left(m).wait_recv()
    band_products(8, 8)
    for m in range(4, 8):
        to_right(m).wait_recv()
        to_left(m).wait_recv()
        on_left(m - 4).start()
    gather_tile(1)
    band_products(16, 8)
    gather_tile(2)
    for q in range(2):
        for m in range(2 * q, 2 * q + 2):
            on_right(m).wait_recv()
            on_left(m).wait_recv()
        band_products(24 + 4 * q, 4)
    gather_tile(3)

    c_copies[1].wait_recv()
    c_copies[2].wait_recv()
    count = row_c[0] + row_c[1] + row_c[2] + row_c[3]
    part = jnp.sum(tiles[0] + tiles[1] + tiles[2] + tiles[3], axis=0, keepdims=True)
    lane1 = lax.broadcasted_iota(jnp.int32, (1, LANES), 1)
    rows[me] = jnp.where(lane1 == LANES - 1, count, part)

    def row_copy(d):
        return pltpu.make_async_remote_copy(
            src_ref=rows.at[me], dst_ref=rows.at[me], send_sem=rsend_sem, recv_sem=rrecv_sem,
            device_id=peer(d), device_id_type=MESH,
        )

    @pl.loop(1, plane)
    def _(d):
        row_copy(d).start()

    far = lax.rem(y + 2, depth)
    t1, t2, t3 = tiles[1], tiles[2], tiles[3]
    mode_ref[y] = tiles[0]
    mode_ref[left, 0:4, :] = t1[0:4]
    mode_ref[left, 4:8, :] = t2[0:4]
    mode_ref[right, 0:4, :] = t1[4:8]
    mode_ref[right, 4:8, :] = t2[4:8]
    mode_ref[far, 0:2, :] = t3[0:2]
    mode_ref[far, 4:6, :] = t3[2:4]
    mode_ref[far, 2:4, :] = t3[4:6]
    mode_ref[far, 6:8, :] = t3[6:8]

    for m in range(own):
        to_right(m).wait_send()
        to_left(m).wait_send()
    for m in range(4):
        on_right(m).wait_send()
        on_left(m).wait_send()
    for c in c_copies:
        c.wait_send()

    others = rows.at[pl.ds(0, plane - 1)]
    pltpu.make_async_copy(others, others, rrecv_sem).wait()
    pltpu.make_async_copy(others, others, rsend_sem).wait()
    whole = jnp.sum(rows[...].reshape(plane, LANES), axis=0, keepdims=True)
    live = jnp.sum(jnp.where(lane1 == LANES - 1, whole, 0.0), axis=1, keepdims=True)
    power_ref[...] = nmax * whole / live


def per_device(observed, eigenvalues, kl_basis, band_deriv, counts):
    own, samples, nmax = observed.shape
    bands, width, _ = band_deriv.shape
    half = width // 2
    depth = lax.axis_size("band")
    plane = lax.axis_size(MA)
    dma = pltpu.SemaphoreType.DMA
    mode, power = pl.pallas_call(
        kernel,
        out_shape=(
            jax.ShapeDtypeStruct((depth, own, LANES), F32),
            jax.ShapeDtypeStruct((1, LANES), F32),
        ),
        in_specs=[pl.BlockSpec(memory_space=pl.ANY)] * 5,
        out_specs=[pl.BlockSpec(memory_space=pltpu.VMEM)] * 2,
        scratch_shapes=[
            pltpu.SMEM((own,), jnp.int32),
            pltpu.VMEM((own, nmax), F32),
            pltpu.VMEM((own, nmax), F32),
            pltpu.VMEM((own, samples, nmax), BF16),
            pltpu.VMEM((own, nmax, width), BF16),
            pltpu.VMEM((bands, width, half), BF16),
            pltpu.VMEM((bands, half, half), BF16),
            pltpu.VMEM((depth * own, samples, width), BF16),
            pltpu.VMEM((bands, depth * own * 8, LANES), F32),
            pltpu.VMEM((depth, own, LANES), F32),
            pltpu.VMEM((depth, 1, LANES), F32),
            pltpu.VMEM((plane, 1, LANES), F32),
            dma((2,)),
            dma((own,)),
            dma((own,)),
            dma((2,)),
            dma((2, 12)),
            dma((32,)),
            dma((3,)),
            dma((4,)),
            dma,
            dma,
        ],
        compiler_params=pltpu.CompilerParams(
            collective_id=0, has_side_effects=True, vmem_limit_bytes=60 * 1024 * 1024
        ),
    )(counts, eigenvalues, observed, kl_basis, band_deriv)
    return mode.reshape(depth * own, LANES)[:, :bands], power[0, :bands]


def solution(mesh):
    split = Mesh(mesh.devices.reshape(4, 4, 2, mesh.shape["band"]), MA_BAND)
    return jax.shard_map(
        per_device,
        mesh=split,
        in_specs=(
            P(MA_BAND, None, None),
            P(MA_BAND, None),
            P(MA_BAND, None, None),
            P("band", None, None),
            P(MA_BAND),
        ),
        out_specs=(P(MA, "band"), P("band")),
        check_vma=False,
    )
```

time: 120 us -> 46 us (0.38); the launches traced: 118 us -> 45.8 us
  Pallas kernels: 0 us -> 42.6 us
  matrix products: 42.1 us -> 0 us
  blocking collectives: 35.5 us -> 0 us
  waiting for transfers between devices: 24.2 us -> 0 us
  starting transfers between devices: 5 us -> 0 us
  other arithmetic: 4.61 us -> 0 us
  local copies, waits for them, and re-layouts: 5.36 us -> 2.53 us
    pallas_call x0 -> x1, Pallas kernels: none -> 42.6 us  [per_device(): pl.pallas_call(kernel, out_shape=(jax.ShapeDtypeStruct((depth, own, LANES...]
    dot_general x11 -> x0, matrix products: 42.1 us -> none  [the longest x10 36.9 us: one_band(): mapped = jnp.dot(flattened, matrix, preferred_element_type=jnp.float32)]
    psum x4 -> x0, blocking collectives: 35.5 us -> none  [over_axes(): x = lax.psum(x, axis)]
    all_to_all x1 -> x0, waiting for transfers between devices: 24.2 us -> none  [from_everyone(): lax.all_to_all(jnp.broadcast_to(x[None], (count, *x.shape)), axis, 0, 0,...]
    all_to_all x1 -> x0, starting transfers between devices: 5 us -> none  [from_everyone(): lax.all_to_all(jnp.broadcast_to(x[None], (count, *x.shape)), axis, 0, 0,...]
    reduce_sum x12 -> x0, other arithmetic: 2.5 us -> none  [the longest x10 1.16 us: one_band(): return jnp.sum((mapped * flattened).reshape(mode_count, -1), axis=1)]
    while x1 -> x0, local copies, waits for them, and re-layouts: 2.47 us -> none  [band_quadratic(): return lax.map(one_band, matrices)]
    broadcast_in_dim x2 -> x0, local copies, waits for them, and re-layouts: 1.59 us -> none  [the longest x1 1.59 us: from_everyone(): jnp.broadcast_to(x[None], (count, *x.shape))]
  transfers between devices with their start and end apart: 1 -> 0, of which waited for: 1 -> 0; matrix products, arithmetic and copies ran while one was open for 1% -> 0% of each run, Pallas kernels for 0% -> 0%
where the time goes in v1:
time: 46 us; the launch traced here: 45.8 us
  Pallas kernels  42.6 us (93%)
  local copies, waits for them, and re-layouts  2.53 us (5%)
  between operations  0.64 us (1%)
    pallas_call x1, Pallas kernels, per_device(): pl.pallas_call(kernel, out_shape=(jax.ShapeDtypeStruct((depth, own, LANES...  42.6 us
    unnamed x1, local copies, waits for them, and re-layouts  1.39 us
    squeeze x1, local copies, waits for them, and re-layouts, per_device(): return (mode.reshape(depth * own, LANES)[:, :bands], power[0, :bands])  1.14 us

profile of v1, /device:TPU:1, one launch (start us, length us, event | category | flops | bytes accessed | tf_op | source)
XLA Modules:
  0.0 45.8 jit_solution(10317230961369400785)
XLA Ops:
  0.6 42.6 %shard_map.68 = (f32[4,8,128]{2,1,0:T(8,128)}, f32[1,128]{1,0:T(1,128)}) custom-call(s32[8]{0:T(128)} %counts_hbm.1, f32[8,1024]{1,0:T(8,128)} %eig_hbm.1, bf16[8,64,1024]{2,1,0:T(8,128)(2,1)} %obs_hbm.1, bf16[8,1024,512]{2,1,0:T(8,128)(2,1)} %kl_hbm.1, bf16[10,512,512]{2,1,0:T(8,128)(2,1)} %d_hbm.1), custom_call_target="tpu_custom_call" | custom-call | tf_op jit(solution)/shard_map/pallas_call | solution.py:237
  43.2 1.4 %copy.8 = f32[32,10]{0,1:T(8,128)} copy(f32[32,10]{1,0:T(8,128)} %bitcast.4) | data formatting | bytes 2560
  44.6 1.1 %slice_bitcast_fusion = f32[10]{0:T(128)} fusion(f32[1,128]{1,0:T(1,128)} %get-tuple-element.5), kind=kLoop, calls=%fused_computation | loop fusion | bytes 80 | tf_op jit(solution)/shard_map/squeeze | solution.py:273

commit v2 on v1

--- a/solution.py
+++ b/solution.py
@@ -19,8 +19,8 @@
 def kernel(
     counts_hbm, eig_hbm, obs_hbm, kl_hbm, d_hbm,
     mode_ref, power_ref,
-    counts_s, eig_v, weight_v, obs_v, kl_v, d1_v, d2_v, vec, acc, tiles, row_c, rows,
-    small_sem, obs_sem, kl_sem, d_sem, send_sem, recv_sem, csend_sem, crecv_sem, rsend_sem, rrecv_sem,
+    counts_s, eig_v, weight_v, obs_v, kl_v, d1_v, d2_v, vec, acc, tiles, order, row_c, rows,
+    small_sem, obs_sem, kl_sem, d_sem, send_sem, recv_sem, csend_sem, crecv_sem, rsend_sem, rrecv_sem, round_sem,
 ):
     own, samples, nmax = obs_v.shape
     bands, width, half = d1_v.shape
@@ -59,12 +59,13 @@
     d2_cp.start()
 
     barrier = pltpu.get_barrier_semaphore()
-    for n in (left, right):
-        pl.semaphore_signal(barrier, inc=1, device_id={"band": n}, device_id_type=MESH)
-
-    @pl.loop(1, plane)
-    def _(d):
-        pl.semaphore_signal(barrier, inc=1, device_id=peer(d), device_id_type=MESH)
+    plane_near = []
+    for axis, at, size in zip(MA, (z, x, core), (nz, nx, nc)):
+        plane_near.append({axis: lax.rem(at + 1, size)})
+        if size > 2:
+            plane_near.append({axis: lax.rem(at + size - 1, size)})
+    for n in [{"band": left}, {"band": right}] + plane_near:
+        pl.semaphore_signal(barrier, inc=1, device_id=n, device_id_type=MESH)
 
     counts_cp.wait()
     eig_cp.wait()
@@ -79,7 +80,12 @@
     weight_v[...] = jnp.where(pos < limit, 1.0 / (1.0 + eig_v[...]), 0.0)
     row_c[0] = jnp.full((1, LANES), total.astype(F32))
 
-    pl.semaphore_wait(barrier, plane + 1)
+    def pass_on(r):
+        for n in plane_near:
+            pl.semaphore_signal(round_sem.at[r], inc=1, device_id=n, device_id_type=MESH)
+
+    def passed_on(r):
+        pl.semaphore_wait(round_sem.at[r], len(plane_near))
 
     def remote(src, dst, s, r, n):
         return pltpu.make_async_remote_copy(
@@ -114,15 +120,26 @@
     def c_copy(s, d, k, n):
         return remote(row_c.at[s], row_c.at[d], csend_sem.at[k], crecv_sem.at[d], n)
 
-    @pl.loop(0, own)
-    def _(m):
+    def project(m):
         obs_cp(m).wait()
         kl_cp(m).wait()
         weighted = (obs_v[m].astype(F32) * weight_v[pl.ds(m, 1), :]).astype(BF16)
         vec[m] = jnp.dot(weighted, kl_v[m], preferred_element_type=F32).astype(BF16)
+
+    project(0)
+    pl.semaphore_wait(barrier, 2 + len(plane_near))
+    to_right(0).start()
+    to_left(0).start()
+    pass_on(0)
+
+    @pl.loop(1, own)
+    def _(m):
+        project(m)
         to_right(m).start()
         to_left(m).start()
 
+    passed_on(0)
+    pass_on(1)
     c_copies = (c_copy(0, 1, 0, right), c_copy(0, 2, 1, left), c_copy(1, 3, 2, right))
     c_copies[0].start()
     c_copies[1].start()
@@ -135,8 +152,10 @@
         d1_v[a, half:, :] = d1_v[a, half:, :] * 2
 
     def band_products(e0, n):
-        @pl.loop(0, bands)
-        def _(a):
+        @pl.loop(0, bands // 5)
+        def _(step):
+          for u in range(5):
+            a = step * 5 + u
             p = vec[e0 : e0 + n].reshape(n * samples, width)
             y1 = jnp.dot(p, d1_v[a], preferred_element_type=F32)
             y2 = jnp.dot(p[:, half:], d2_v[a], preferred_element_type=F32)
@@ -158,6 +177,8 @@
         tiles[g] = t
 
     band_products(0, 8)
+    passed_on(1)
+    pass_on(2)
     gather_tile(0)
 
     c_copies[0].wait_recv()
@@ -167,12 +188,15 @@
         on_right(m).start()
         to_left(m).wait_recv()
     band_products(8, 8)
+    passed_on(2)
+    pass_on(3)
     for m in range(4, 8):
         to_right(m).wait_recv()
         to_left(m).wait_recv()
         on_left(m - 4).start()
     gather_tile(1)
     band_products(16, 8)
+    passed_on(3)
     gather_tile(2)
     for q in range(2):
         for m in range(2 * q, 2 * q + 2):
@@ -200,15 +224,16 @@
 
     far = lax.rem(y + 2, depth)
     t1, t2, t3 = tiles[1], tiles[2], tiles[3]
-    mode_ref[y] = tiles[0]
-    mode_ref[left, 0:4, :] = t1[0:4]
-    mode_ref[left, 4:8, :] = t2[0:4]
-    mode_ref[right, 0:4, :] = t1[4:8]
-    mode_ref[right, 4:8, :] = t2[4:8]
-    mode_ref[far, 0:2, :] = t3[0:2]
-    mode_ref[far, 4:6, :] = t3[2:4]
-    mode_ref[far, 2:4, :] = t3[4:6]
-    mode_ref[far, 6:8, :] = t3[6:8]
+    order[y] = tiles[0]
+    order[left, 0:4, :] = t1[0:4]
+    order[left, 4:8, :] = t2[0:4]
+    order[right, 0:4, :] = t1[4:8]
+    order[right, 4:8, :] = t2[4:8]
+    order[far, 0:2, :] = t3[0:2]
+    order[far, 4:6, :] = t3[2:4]
+    order[far, 2:4, :] = t3[4:6]
+    order[far, 6:8, :] = t3[6:8]
+    mode_ref[...] = jnp.transpose(order[...].reshape(depth * own, LANES))[0:bands, :]
 
     for m in range(own):
         to_right(m).wait_send()
@@ -225,6 +250,11 @@
     whole = jnp.sum(rows[...].reshape(plane, LANES), axis=0, keepdims=True)
     live = jnp.sum(jnp.where(lane1 == LANES - 1, whole, 0.0), axis=1, keepdims=True)
     power_ref[...] = nmax * whole / live
+
+
+def results(mode_ref, power_ref, mode_out, power_out):
+    mode_out[...] = mode_ref[...]
+    power_out[...] = power_ref[0, : power_out.shape[0]]
 
 
 def per_device(observed, eigenvalues, kl_basis, band_deriv, counts):
@@ -237,10 +267,10 @@
     mode, power = pl.pallas_call(
         kernel,
         out_shape=(
-            jax.ShapeDtypeStruct((depth, own, LANES), F32),
+            jax.ShapeDtypeStruct((bands, depth * own), F32),
             jax.ShapeDtypeStruct((1, LANES), F32),
         ),
-        in_specs=[pl.BlockSpec(memory_space=pl.ANY)] * 5,
+        in_specs=[pl.BlockSpec(memory_space=pltpu.HBM)] * 5,
         out_specs=[pl.BlockSpec(memory_space=pltpu.VMEM)] * 2,
         scratch_shapes=[
             pltpu.SMEM((own,), jnp.int32),
@@ -252,6 +282,7 @@
             pltpu.VMEM((bands, half, half), BF16),
             pltpu.VMEM((depth * own, samples, width), BF16),
             pltpu.VMEM((bands, depth * own * 8, LANES), F32),
+            pltpu.VMEM((depth, own, LANES), F32),
             pltpu.VMEM((depth, own, LANES), F32),
             pltpu.VMEM((depth, 1, LANES), F32),
             pltpu.VMEM((plane, 1, LANES), F32),
@@ -265,12 +296,17 @@
             dma((4,)),
             dma,
             dma,
+            pltpu.SemaphoreType.REGULAR((4,)),
         ],
         compiler_params=pltpu.CompilerParams(
-            collective_id=0, has_side_effects=True, vmem_limit_bytes=60 * 1024 * 1024
+            collective_id=0, has_side_effects=True, vmem_limit_bytes=63 * 1024 * 1024
         ),
     )(counts, eigenvalues, observed, kl_basis, band_deriv)
-    return mode.reshape(depth * own, LANES)[:, :bands], power[0, :bands]
+    mode, power = pl.pallas_call(
+        results,
+        out_shape=(jax.ShapeDtypeStruct(mode.shape, F32), jax.ShapeDtypeStruct((bands,), F32)),
+    )(mode, power)
+    return mode.T, power
 
 
 def solution(mesh):

time: 46 us -> 38.9 us (0.85)
  Pallas kernels: 42.6 us -> 38.1 us
  local copies, waits for them, and re-layouts: 2.53 us -> 0 us
    pallas_call x1 -> x2, Pallas kernels: 42.6 us -> 38.1 us  [the longest x1 36.8 us: per_device(): pl.pallas_call(kernel, out_shape=(jax.ShapeDtypeStruct((bands, depth * ow...]
    unnamed x1 -> x0, local copies, waits for them, and re-layouts: 1.39 us -> none
    squeeze x1 -> x0, local copies, waits for them, and re-layouts: 1.14 us -> none  [per_device(): return (mode.reshape(depth * own, LANES)[:, :bands], power[0, :bands])]
where the time goes in v2:
time: 38.9 us; the launch traced here: 38.7 us
  Pallas kernels  38.1 us (98%)
  between operations  0.64 us (2%)
    pallas_call x1, Pallas kernels, per_device(): pl.pallas_call(kernel, out_shape=(jax.ShapeDtypeStruct((bands, depth * ow...  36.8 us
    pallas_call x1, Pallas kernels, per_device(): pl.pallas_call(results, out_shape=(jax.ShapeDtypeStruct(mode.shape, F32),...  1.3 us

profile of v2, /device:TPU:1, one launch (start us, length us, event | category | flops | bytes accessed | tf_op | source)
XLA Modules:
  0.0 38.7 jit_solution(7254353225318119251)
XLA Ops:
  0.6 36.8 %shard_map.68 = (f32[10,32]{1,0:T(8,128)}, f32[1,128]{1,0:T(1,128)}) custom-call(s32[8]{0:T(128)} %counts_hbm.1, f32[8,1024]{1,0:T(8,128)} %eig_hbm.1, bf16[8,64,1024]{2,1,0:T(8,128)(2,1)} %obs_hbm.1, bf16[8,1024,512]{2,1,0:T(8,128)(2,1)} %kl_hbm.1, bf16[10,512,512]{2,1,0:T(8,128)(2,1)} %d_hbm.1), custom_call_target="tpu_custom_call" | custom-call | tf_op jit(solution)/shard_map/pallas_call | solution.py:267
  37.4 1.3 %shard_map.69 = (f32[10,32]{1,0:T(8,128)}, f32[10]{0:T(128)}) custom-call(f32[10,32]{1,0:T(8,128)} %get-tuple-element.6.mode_ref, f32[1,128]{1,0:T(1,128)} %get-tuple-element.7.power_ref), custom_call_target="tpu_custom_call" | custom-call | tf_op jit(solution)/shard_map/pallas_call | solution.py:305

commit v3 on v2

v3 whole, which is shorter than its diff:
```python
import functools

import jax
import jax.numpy as jnp
from jax import lax
from jax.experimental import pallas as pl
from jax.experimental.pallas import tpu as pltpu
from jax.sharding import Mesh
from jax.sharding import PartitionSpec as P

MA = ("ma_0", "ma_1", "ma_2")
MA_BAND = MA + ("band",)
MESH = pl.DeviceIdType.MESH
LANES = 128
F32 = jnp.float32
BF16 = jnp.bfloat16
FAR = ((0, 4), (4, 6), (6, 8))


def kernel(
    counts_hbm, eig_hbm, obs_hbm, kl_hbm, d_hbm,
    mode_ref, power_ref,
    counts_s, eig_v, weight_v, obs_v, kl_v, d1_v, d2_v, vec, acc, tiles, order, row_c, rows,
    small_sem, load_sem, d_sem, send_sem, recv_sem, far_sem, csend_sem, crecv_sem, rsend_sem, rrecv_sem, round_sem,
):
    own, samples, nmax = obs_v.shape
    bands, width, half = d1_v.shape
    depth = lax.axis_size("band")
    z, x, core = (lax.axis_index(a) for a in MA)
    nz, nx, nc = (lax.axis_size(a) for a in MA)
    plane = nz * nx * nc
    me = (z * nx + x) * nc + core
    y = lax.axis_index("band")
    right = lax.rem(y + 1, depth)
    left = lax.rem(y + depth - 1, depth)

    def obs_cp(m):
        return pltpu.make_async_copy(obs_hbm.at[m], obs_v.at[m], load_sem.at[2 * m])

    def kl_cp(m):
        return pltpu.make_async_copy(kl_hbm.at[m], kl_v.at[m], load_sem.at[2 * m + 1])

    counts_cp = pltpu.make_async_copy(counts_hbm, counts_s, small_sem.at[0])
    eig_cp = pltpu.make_async_copy(eig_hbm, eig_v, small_sem.at[1])
    counts_cp.start()
    kl_cp(0).start()
    obs_cp(0).start()
    eig_cp.start()

    @pl.loop(1, own)
    def _(m):
        obs_cp(m).start()
        kl_cp(m).start()

    d1_cp = pltpu.make_async_copy(d_hbm.at[:, :, pl.ds(0, half)], d1_v, d_sem.at[0])
    d2_cp = pltpu.make_async_copy(d_hbm.at[:, pl.ds(half, half), pl.ds(half, half)], d2_v, d_sem.at[1])
    d1_cp.start()
    d2_cp.start()

    barrier = pltpu.get_barrier_semaphore()
    plane_near = []
    for axis, at, size in zip(MA, (z, x, core), (nz, nx, nc)):
        plane_near.append({axis: lax.rem(at + 1, size)})
        if size > 2:
            plane_near.append({axis: lax.rem(at + size - 1, size)})
    for n in [{"band": left}, {"band": right}] + plane_near:
        pl.semaphore_signal(barrier, inc=1, device_id=n, device_id_type=MESH)

    counts_cp.wait()
    eig_cp.wait()
    sub = lax.broadcasted_iota(jnp.int32, (own, nmax), 0)
    pos = lax.broadcasted_iota(jnp.int32, (own, nmax), 1)
    limit = jnp.zeros((own, nmax), jnp.int32)
    total = counts_s[0]
    for m in range(own):
        limit = jnp.where(sub == m, counts_s[m], limit)
        if m:
            total = total + counts_s[m]
    weight_v[...] = jnp.where(pos < limit, 1.0 / (1.0 + eig_v[...]), 0.0)
    row_c[0] = jnp.full((1, LANES), total.astype(F32))

    def pass_on(r):
        for n in plane_near:
            pl.semaphore_signal(round_sem.at[r], inc=1, device_id=n, device_id_type=MESH)

    def passed_on(r):
        pl.semaphore_wait(round_sem.at[r], len(plane_near))

    def remote(src, dst, s, r, n):
        return pltpu.make_async_remote_copy(
            src_ref=src, dst_ref=dst, send_sem=s, recv_sem=r, device_id={"band": n}, device_id_type=MESH
        )

    def e_left(m):
        return 8 + (m // 2) * 4 + lax.rem(m, 2)

    def e_right(m):
        return 10 + (m // 2) * 4 + lax.rem(m, 2)

    def to_right(m):
        return remote(vec.at[m], vec.at[e_left(m)], send_sem, recv_sem.at[0, m // 2], right)

    def to_left(m):
        return remote(vec.at[m], vec.at[e_right(m)], send_sem, recv_sem.at[1, m // 2], left)

    def on_right(m, step):
        src = vec.at[e_left(m), pl.ds(0, samples // 2)]
        return remote(src, vec.at[24 + m, pl.ds(0, samples // 2)], send_sem, far_sem.at[step], right)

    def on_left(m, step):
        rest = pl.ds(samples // 2, samples // 2)
        return remote(vec.at[e_right(m), rest], vec.at[24 + m, rest], send_sem, far_sem.at[step], left)

    def arrived(e, n, sem):
        landed = vec.at[pl.ds(e, n)]
        pltpu.make_async_copy(landed, landed, sem).wait()

    def c_copy(s, d, k, n):
        return remote(row_c.at[s], row_c.at[d], csend_sem, crecv_sem.at[k], n)

    def project(m):
        obs_cp(m).wait()
        kl_cp(m).wait()
        weighted = (obs_v[m].astype(F32) * weight_v[pl.ds(m, 1), :]).astype(BF16)
        vec[m] = jnp.dot(weighted, kl_v[m], preferred_element_type=F32).astype(BF16)

    project(0)
    pl.semaphore_wait(barrier, 2 + len(plane_near))
    c_copies = (c_copy(0, 1, 0, right), c_copy(0, 2, 1, left), c_copy(1, 3, 1, right))
    c_copies[0].start()
    c_copies[1].start()
    to_right(0).start()
    to_left(0).start()
    pass_on(0)

    @pl.loop(1, own)
    def _(m):
        project(m)
        to_right(m).start()
        to_left(m).start()

    d1_cp.wait()
    d2_cp.wait()

    @pl.loop(0, bands)
    def _(a):
        d1_v[a, half:, :] = d1_v[a, half:, :] * 2

    def band_products(e0, n):
        unroll = bands if n <= 2 else 5

        @pl.loop(0, bands // unroll)
        def _(step):
          for u in range(unroll):
            a = step * unroll + u
            p = vec[e0 : e0 + n].reshape(n * samples, width)
            y1 = jnp.dot(p, d1_v[a], preferred_element_type=F32)
            y2 = jnp.dot(p[:, half:], d2_v[a], preferred_element_type=F32)
            q = y1 * p[:, :half].astype(F32) + y2 * p[:, half:].astype(F32)
            q = q[:, :LANES] + q[:, LANES:]
            q = jnp.sum(q.reshape(n, samples // 8, 8, LANES), axis=1)
            acc[a, e0 * 8 : (e0 + n) * 8, :] = q.reshape(n * 8, LANES)

    lane = lax.broadcasted_iota(jnp.int32, (8, LANES), 1)

    def gather_tile(g):
        t = jnp.zeros((8, LANES), F32)
        for a in range(bands):
            v = acc[a, pl.ds(g * 64, 8, stride=8), :]
            for k in range(1, 8):
                v = v + acc[a, pl.ds(g * 64 + k, 8, stride=8), :]
            t = jnp.where(lane == a, jnp.sum(v, axis=1, keepdims=True), t)
        tiles[g] = t / samples

    step_of = {m: i for i, (m0, m1) in enumerate(FAR) for m in range(m0, m1)}

    def from_both(pair):
        modes = (2 * pair, 2 * pair + 1)
        arrived(8 + 4 * pair, 2, recv_sem.at[0, pair])
        for m in modes:
            on_right(m, step_of[m]).start()
        arrived(10 + 4 * pair, 2, recv_sem.at[1, pair])
        for m in modes:
            on_left(m, step_of[m]).start()

    band_products(0, 8)
    passed_on(0)
    pass_on(1)
    gather_tile(0)
    from_both(0)
    from_both(1)
    band_products(8, 8)
    passed_on(1)
    pass_on(2)
    c_copies[0].wait_recv()
    c_copies[2].start()
    gather_tile(1)
    from_both(2)
    band_products(16, 4)
    from_both(3)
    passed_on(2)
    pass_on(3)
    band_products(20, 4)
    gather_tile(2)
    near = tiles[0] + tiles[1] + tiles[2]
    for step, (m0, m1) in enumerate(FAR):
        arrived(24 + m0, m1 - m0, far_sem.at[step])
        band_products(24 + m0, m1 - m0)
    gather_tile(3)
    passed_on(3)

    rest_c = row_c.at[pl.ds(2, 2)]
    pltpu.make_async_copy(rest_c, rest_c, crecv_sem.at[1]).wait()
    count = row_c[0] + row_c[1] + row_c[2] + row_c[3]
    part = jnp.sum(near + tiles[3], axis=0, keepdims=True)
    lane1 = lax.broadcasted_iota(jnp.int32, (1, LANES), 1)
    rows[me] = jnp.where(lane1 == LANES - 1, count, part)

    shifts = [(a, b, c) for a in range(nz) for b in range(nx) for c in range(nc)]
    shifts.sort(key=lambda s: -(min(s[0], nz - s[0]) + min(s[1], nx - s[1])))
    zs, xs, cs = ([lax.rem(at + i, n) for i in range(n)] for at, n in ((z, nz), (x, nx), (core, nc)))
    for a, b, c in shifts:
        if a or b or c:
            pltpu.make_async_remote_copy(
                src_ref=rows.at[me], dst_ref=rows.at[me], send_sem=rsend_sem, recv_sem=rrecv_sem,
                device_id=dict(zip(MA, (zs[a], xs[b], cs[c]))), device_id_type=MESH,
            ).start()

    far = lax.rem(y + 2, depth)
    order[y] = tiles[0]
    for c in range(2):
        t = tiles[1 + c]
        order[left, 4 * c : 4 * c + 2, :] = t[0:2]
        order[left, 4 * c + 2 : 4 * c + 4, :] = t[4:6]
        order[right, 4 * c : 4 * c + 2, :] = t[2:4]
        order[right, 4 * c + 2 : 4 * c + 4, :] = t[6:8]
    order[far] = tiles[3]
    mode_ref[...] = jnp.transpose(order[...].reshape(depth * own, LANES))[0:bands, :]

    sent = vec.at[pl.ds(0, 3 * own)]
    pltpu.make_async_copy(sent, sent, send_sem).wait()
    rows_c = row_c.at[pl.ds(0, 3)]
    pltpu.make_async_copy(rows_c, rows_c, csend_sem).wait()
    others = rows.at[pl.ds(0, plane - 1)]
    pltpu.make_async_copy(others, others, rsend_sem).wait()
    pltpu.make_async_copy(others, others, rrecv_sem).wait()
    whole = jnp.sum(rows[...].reshape(plane, LANES), axis=0, keepdims=True)
    live = jnp.sum(jnp.where(lane1 == LANES - 1, whole, 0.0), axis=1, keepdims=True)
    power_ref[...] = (nmax * whole / live)[0, :bands]


def results(mode_ref, power_ref, mode_out, power_out, sems):
    copies = (
        pltpu.make_async_copy(mode_ref, mode_out, sems.at[0]),
        pltpu.make_async_copy(power_ref, power_out, sems.at[1]),
    )
    for c in copies:
        c.start()
    for c in copies:
        c.wait()


def per_device(observed, eigenvalues, kl_basis, band_deriv, counts):
    own, samples, nmax = observed.shape
    bands, width, _ = band_deriv.shape
    half = width // 2
    depth = lax.axis_size("band")
    plane = lax.axis_size(MA)
    dma = pltpu.SemaphoreType.DMA
    counts, eigenvalues, observed, kl_basis, band_deriv = (
        pltpu.with_memory_space_constraint(v, pltpu.HBM)
        for v in (counts, eigenvalues, observed, kl_basis, band_deriv)
    )
    mode, power = pl.pallas_call(
        kernel,
        out_shape=(
            jax.ShapeDtypeStruct((bands, depth * own), F32),
            jax.ShapeDtypeStruct((bands,), F32),
        ),
        in_specs=[pl.BlockSpec(memory_space=pltpu.HBM)] * 5,
        out_specs=[pl.BlockSpec(memory_space=pltpu.VMEM)] * 2,
        scratch_shapes=[
            pltpu.SMEM((own,), jnp.int32),
            pltpu.VMEM((own, nmax), F32),
            pltpu.VMEM((own, nmax), F32),
            pltpu.VMEM((own, samples, nmax), BF16),
            pltpu.VMEM((own, nmax, width), BF16),
            pltpu.VMEM((bands, width, half), BF16),
            pltpu.VMEM((bands, half, half), BF16),
            pltpu.VMEM((depth * own, samples, width), BF16),
            pltpu.VMEM((bands, depth * own * 8, LANES), F32),
            pltpu.VMEM((depth, own, LANES), F32),
            pltpu.VMEM((depth, own, LANES), F32),
            pltpu.VMEM((depth, 1, LANES), F32),
            pltpu.VMEM((plane, 1, LANES), F32),
            dma((2,)),
            dma((2 * own,)),
            dma((2,)),
            dma,
            dma((2, own // 2)),
            dma((len(FAR),)),
            dma,
            dma((2,)),
            dma,
            dma,
            pltpu.SemaphoreType.REGULAR((4,)),
        ],
        compiler_params=pltpu.CompilerParams(
            collective_id=0, has_side_effects=True, vmem_limit_bytes=50 * 1024 * 1024
        ),
    )(counts, eigenvalues, observed, kl_basis, band_deriv)
    mode, power = (pltpu.with_memory_space_constraint(v, pltpu.VMEM) for v in (mode, power))
    mode, power = pl.pallas_call(
        results,
        out_shape=(jax.ShapeDtypeStruct(mode.shape, F32), jax.ShapeDtypeStruct(power.shape, F32)),
        in_specs=[pl.BlockSpec(memory_space=pltpu.VMEM)] * 2,
        out_specs=[pl.BlockSpec(memory_space=pl.ANY)] * 2,
        scratch_shapes=[dma((2,))],
    )(mode, power)
    return mode.T, power


def solution(mesh):
    split = Mesh(mesh.devices.reshape(4, 4, 2, mesh.shape["band"]), MA_BAND)
    return jax.shard_map(
        per_device,
        mesh=split,
        in_specs=(
            P(MA_BAND, None, None),
            P(MA_BAND, None),
            P(MA_BAND, None, None),
            P("band", None, None),
            P(MA_BAND),
        ),
        out_specs=(P(MA, "band"), P("band")),
        check_vma=False,
    )
```

time: 38.9 us -> 33.8 us (0.87)
  Pallas kernels: 38.1 us -> 33.1 us
    pallas_call x1, Pallas kernels: 36.8 us -> 32.5 us  [per_device(): pl.pallas_call(kernel, out_shape=(jax.ShapeDtypeStruct((bands, depth * ow...]
    pallas_call x1, Pallas kernels: 1.3 us -> 0.61 us  [per_device(): pl.pallas_call(results, out_shape=(jax.ShapeDtypeStruct(mode.shape, F32),...]
where the time goes in v3:
time: 33.8 us; the launch traced here: 33.7 us
  Pallas kernels  33.1 us (98%)
  between operations  0.64 us (2%)
    pallas_call x1, Pallas kernels, per_device(): pl.pallas_call(kernel, out_shape=(jax.ShapeDtypeStruct((bands, depth * ow...  32.5 us

profile of v3, /device:TPU:1, one launch (start us, length us, event | category | flops | bytes accessed | tf_op | source)
XLA Modules:
  0.0 33.7 jit_solution(13435180161743331824)
XLA Ops:
  0.6 32.5 %shard_map.68 = (f32[10,32]{1,0:T(8,128)S(1)}, f32[10]{0:T(128)S(1)}) custom-call(s32[8]{0:T(128)} %counts_hbm.1, f32[8,1024]{1,0:T(8,128)} %eig_hbm.1, bf16[8,64,1024]{2,1,0:T(8,128)(2,1)} %obs_hbm.1, bf16[8,1024,512]{2,1,0:T(8,128)(2,1)} %kl_hbm.1, bf16[10,512,512]{2,1,0:T(8,128)(2,1)} %d_hbm.1), custom_call_target="tpu_custom_call" | custom-call | tf_op jit(solution)/shard_map/pallas_call | solution.py:274
  33.1 0.6 %shard_map.69 = (f32[10,32]{1,0:T(8,128)}, f32[10]{0:T(128)}) custom-call(f32[10,32]{1,0:T(8,128)S(1)} %get-tuple-element.6.mode_ref, f32[10]{0:T(128)S(1)} %get-tuple-element.7.power_ref), custom_call_target="tpu_custom_call" | custom-call | tf_op jit(solution)/shard_map/pallas_call | solution.py:313
